TPU v7x, 128 devices: a whole 4x4x4 slice. The times are simulated.
128 devices in a mesh: vec: 8 (over y, z_lo), gz: 16 (over x, z_hi, core).
Axes of the slice: x: 4, y: 4, z: 4 (z_hi: 2, z_lo: 2; z = z_hi * 2 + z_lo), core: 2. Of those that a mesh axis runs over, the one named last changes fastest.
Arguments:
- vectors: bfloat16 [1024, 3, 2, 8192], P('vec', None, None, 'gz'), may hold values from -6 to 6
- links: float32 [3, 3, 3, 2, 8192], P(None, None, None, None, 'gz'), may hold values from -4 to 4
- dirs: int32 [6], replicated, may hold values from 0 to 5, each once
- moms: int32 [2, 3], replicated, may hold values from -2 to 2
Outputs:
- elementals: float32 [6, 2, 2, 1024, 1024], P(None, None, None, ('vec', 'gz'))
Inputs may be any that keep to these rules, and one draw needn't show every extreme that they name: `dirs`: each of the six directions appears exactly once.
All inputs are finite; a program needn't handle non-finite values.
Results may differ from a plain program's by a relative error of at most 0.0039.
Values may be sent and summed in bfloat16 or wider, within the bound.
A program may use at most 192 MiB of HBM per device.

v0:
```python
import math
import jax
import jax.numpy as jnp
from jax import lax
from jax.sharding import PartitionSpec as P

LX = 32
LY = 8


def from_behind(shard, axis, by):
    peers = lax.axis_size(axis)
    return lax.ppermute(shard, axis, [(i, (i + by) % peers) for i in range(peers)])


def extended_2(cells, sides, width):
    for axis, dim in sides:
        count = lax.axis_size(axis)
        head = lax.slice_in_dim(cells, 0, width, axis=dim)
        tail = lax.slice_in_dim(cells, cells.shape[dim] - width, cells.shape[dim], axis=dim)
        cells = jnp.concatenate(
            [
                lax.ppermute(tail, axis, [(i, (i + 1) % count) for i in range(count)]),
                cells,
                lax.ppermute(head, axis, [((i + 1) % count, i) for i in range(count)]),
            ],
            axis=dim,
        )
    return cells


def split_up(shard, dim, peers):
    before, after = (shard.shape[:dim], shard.shape[dim + 1 :])
    return jnp.moveaxis(shard.reshape(*before, peers, -1, *after), dim, 0)


def sum_at_owner(shard, axis, dim):
    blocks = split_up(shard, dim, lax.axis_size(axis))
    arrived = lax.all_to_all(blocks, axis, split_axis=0, concat_axis=0, tiled=True)
    return arrived.sum(axis=0)


def colour_apply(link_real, link_imag, vec_real, vec_imag):
    out_real = jnp.float32(0.0)
    out_imag = jnp.float32(0.0)
    for column in range(3):
        left_real = link_real[None, :, column]
        left_imag = link_imag[None, :, column]
        right_real = vec_real[:, None, column].astype(jnp.float32)
        right_imag = vec_imag[:, None, column].astype(jnp.float32)
        out_real = out_real + left_real * right_real - left_imag * right_imag
        out_imag = out_imag + left_real * right_imag + left_imag * right_real
    return (out_real, out_imag)


def neighbour(field, stride, extent, position, forward):
    if forward:
        inside = jnp.roll(field, -stride, axis=-1)
        beside_all = jnp.roll(field, (extent - 1) * stride, axis=-1)
        return jnp.where(position == extent - 1, beside_all, inside)
    inside = jnp.roll(field, stride, axis=-1)
    beside_all = jnp.roll(field, -(extent - 1) * stride, axis=-1)
    return jnp.where(position == 0, beside_all, inside)


def displace(extended, links, lower_links, direction, plane, x_index, y_index):
    sites = links.shape[-1]
    axis_index = direction % 3
    link = links[axis_index]
    if direction < 3:
        if axis_index == 0:
            moved = neighbour(extended[..., plane : plane + sites], 1, LX, x_index, True)
        elif axis_index == 1:
            moved = neighbour(extended[..., plane : plane + sites], LX, LY, y_index, True)
        else:
            moved = extended[..., 2 * plane : 2 * plane + sites]
        link_real = link[:, :, 0]
        link_imag = link[:, :, 1]
    else:
        if axis_index == 0:
            moved = neighbour(extended[..., plane : plane + sites], 1, LX, x_index, False)
            behind = neighbour(link, 1, LX, x_index, False)
        elif axis_index == 1:
            moved = neighbour(extended[..., plane : plane + sites], LX, LY, y_index, False)
            behind = neighbour(link, LX, LY, y_index, False)
        else:
            moved = extended[..., 0:sites]
            behind = jnp.concatenate((lower_links, link), axis=-1)[..., 0:sites]
        link_real = jnp.swapaxes(behind[:, :, 0], 0, 1)
        link_imag = -jnp.swapaxes(behind[:, :, 1], 0, 1)
    disp_real, disp_imag = colour_apply(link_real, link_imag, moved[:, :, 0], moved[:, :, 1])
    return jnp.stack((disp_real.astype(jnp.bfloat16), disp_imag.astype(jnp.bfloat16)), axis=2)


def on_device(vectors, links, dirs, moms):
    sites = vectors.shape[-1]
    plane = LY * LX
    depth = sites // plane
    shards = lax.axis_size("gz")
    flat = jnp.arange(sites, dtype=jnp.int32)
    x_index = flat % LX
    y_index = flat // LX % LY
    z_index = lax.axis_index("gz") * depth + flat // plane
    lower_links = from_behind(links[2, :, :, :, sites - plane :], "gz", 1)
    gathered = lax.all_gather(vectors, "vec", axis=0, tiled=True)
    extended = extended_2(gathered, (("gz", 3),), plane)
    momenta = moms.astype(jnp.float32)
    theta = (
        momenta[:, 0, None] * x_index.astype(jnp.float32) / LX
        + momenta[:, 1, None] * y_index.astype(jnp.float32) / LY
        + momenta[:, 2, None] * z_index.astype(jnp.float32) / (depth * shards)
    ) * (2.0 * math.pi)
    cosine = jnp.cos(theta)[:, None, None]
    sine = jnp.sin(theta)[:, None, None]
    own_f = vectors.astype(jnp.float32)
    real_part = own_f[:, :, 0][None]
    imag_part = own_f[:, :, 1][None]
    phased_real = (cosine * real_part - sine * imag_part).astype(jnp.bfloat16)
    phased_imag = (sine * real_part + cosine * imag_part).astype(jnp.bfloat16)
    left_side = jnp.stack(
        (
            jnp.stack((phased_real, phased_imag), axis=3),
            jnp.stack((-phased_imag, phased_real), axis=3),
        ),
        axis=0,
    )
    terms = []
    for direction in range(6):
        displaced = displace(extended, links, lower_links, direction, plane, x_index, y_index)
        product = jnp.einsum(
            "qpicrs,jcrs->pqij", left_side, displaced, preferred_element_type=jnp.float32
        )
        terms.append(sum_at_owner(product, "gz", 2))
    stacked = jnp.stack(terms, axis=0)
    select = (dirs[:, None] == jnp.arange(6, dtype=jnp.int32)[None, :]).astype(jnp.float32)
    chosen = jnp.einsum("dk,kpqij->dpqij", select, stacked, precision=lax.Precision.HIGHEST)
    return chosen * (1.0 / math.sqrt(3.0 * sites * shards))


def solution(mesh):
    placed = (P("vec", None, None, "gz"), P(None, None, None, None, "gz"), P(), P())
    return jax.shard_map(
        on_device,
        mesh=mesh,
        in_specs=placed,
        out_specs=P(None, None, None, ("vec", "gz"), None),
        check_vma=False,
    )
```

profile of v0, /device:TPU:40, one launch (start us, length us, event | category | flops | bytes accessed | tf_op | source)
XLA Modules:
  0.0 507.7 jit_solution(9093775337054759167)
XLA Ops:
  6.5 2.3 copy_convert_fusion
  12.6 1.9 maximum_bitcast_fusion.24
  21.5 120.3 %all-gather.2.cloned.1.call-done = bf16[1024,3,2,512]{3,0,2,1:T(8,128)(2,1)} async-done(((bf16[128,3,2,512]{3,0,2,1:T(8,128)(2,1)}), bf16[1024,3,2,512]{3,0,2,1:T(8,128)(2,1)}) %all-gather.2.cloned.1.call-update) | async-done | bytes 6291472 | tf_op jit(solution)/shard_map/all_gather | solution.py:105
  141.8 7.9 %fusion.92 = (bf16[1024,3,2,481]{3,0,2,1:T(8,128)(2,1)S(1)}, bf16[1024,3,2,481]{3,0,2,1:T(8,128)(2,1)S(1)}) fusion(bf16[1024,3,2,512]{3,0,2,1:T(8,128)(2,1)} %all-gather.2.cloned.1.call-done), kind=kLoop, calls=%fused_computation.256 | loop fusion | bytes 23642112 | tf_op jit(solution)/shard_map/jit(_roll_static)/slice | solution.py:62
  149.7 1.9 fusion.93
  151.5 2.5 fusion.90
  154.0 5.0 fusion.91
  159.0 17.8 %maximum_select_fusion = (bf16[1024,3,2,512]{3,0,2,1:T(8,128)(2,1)}, bf16[1024,3,2,512]{3,0,2,1:T(8,128)(2,1)}) fusion(bf16[1024,3,2,481]{3,0,2,1:T(8,128)(2,1)S(1)} %get-tuple-element.49, bf16[1024,3,2,31]{3,0,2,1:T(8,128)(2,1)} %get-tuple-element.51, bf16[1024,3,2,1]{3,0,2,1:T(8,128)(2,1)} %get-tuple-element.45, ...), kind=kLoop, calls=%fused_computation | loop fusion | flops 56623104 | bytes 37749760 | tf_op jit(solution)/shard_map/jit(_where)/select_n | solution.py:60
  176.8 3.3 slice_bitcast_fusion.11
  181.6 4.9 subtract_convert_fusion.5
  186.6 3.4 fusion.23
  191.5 6.5 %all-to-all-start = ((f32[16,2,2,8,1024]{4,3,1,2,0:T(8,128)}), f32[16,2,2,8,1024]{4,3,1,2,0:T(8,128)}, u32[]{:S(2)}, u32[]{:S(2)}) async-start(f32[16,2,2,8,1024]{4,3,1,2,0:T(8,128)} %bitcast.488), calls=%async_computation | async-start | bytes 4194304 | tf_op jit(solution)/shard_map/all_to_all | solution.py:39
  198.0 10.2 %fusion.88 = (bf16[1024,3,2,288]{3,0,2,1:T(8,128)(2,1)}, bf16[1024,3,2,288]{3,0,2,1:T(8,128)(2,1)}) fusion(bf16[1024,3,2,512]{3,0,2,1:T(8,128)(2,1)} %all-gather.2.cloned.1.call-done), kind=kLoop, calls=%fused_computation.252 | loop fusion | bytes 14155776 | tf_op jit(solution)/shard_map/jit(_roll_static)/slice | solution.py:62
  208.2 4.4 fusion.89
  212.7 1.9 fusion.86
  214.5 6.4 %fusion.87 = (bf16[1024,3,2,480]{3,0,2,1:T(8,128)(2,1)}, bf16[1024,3,2,480]{3,0,2,1:T(8,128)(2,1)}) fusion(bf16[1024,3,2,512]{3,0,2,1:T(8,128)(2,1)S(1)} %bitcast.481), kind=kLoop, calls=%fused_computation.251 | loop fusion | bytes 23592960 | tf_op jit(solution)/shard_map/jit(_roll_static)/slice | solution.py:61
  221.0 17.1 %maximum_select_fusion.1 = (bf16[1024,3,2,512]{3,0,2,1:T(8,128)(2,1)}, bf16[1024,3,2,512]{3,0,2,1:T(8,128)(2,1)S(1)}) fusion(bf16[1024,3,2,288]{3,0,2,1:T(8,128)(2,1)} %get-tuple-element.39, bf16[1024,3,2,224]{3,0,2,1:T(8,128)(2,1)} %get-tuple-element.41, bf16[1024,3,2,32]{3,0,2,1:T(8,128)(2,1)} %get-tuple-element.35, ...), kind=kLoop, calls=%fused_computation.5 | loop fusion | flops 56623104 | bytes 37749760 | tf_op jit(solution)/shard_map/jit(_where)/select_n | solution.py:60
  238.1 3.3 slice_bitcast_fusion.9
  242.5 5.3 %subtract_convert_fusion.4 = (bf16[1024,3,1,512]{3,0,2,1:T(8,128)(2,1)S(1)}, bf16[1024,3,1,512]{3,0,2,1:T(8,128)(2,1)S(1)}) fusion(f32[1024,512]{1,0:T(8,128)S(1)} %get-tuple-element.84, f32[3,512]{1,0:T(4,128)S(1)} %bitcast.513, f32[1024,512]{1,0:T(8,128)S(1)} %get-tuple-element.81, f32[3,512]{1,0:T(4,128)S(1)} %bitcast.514, ...), kind=kLoop, calls=%fused_computation.37 | loop fusion | flops 37748736 | bytes 18911232 | tf_op jit(solution)/shard_map/convert_element_type | solution.py:92
  247.8 4.8 fusion.22
  254.3 3.2 fusion.85
  258.0 4.9 collective-permute-start
  263.9 2.0 fusion.41
  265.9 2.0 slice_bitcast_fusion.3
  268.1 4.9 subtract_convert_fusion.2
  273.0 3.4 fusion.20
  277.9 5.4 %all-to-all-start.1 = ((f32[16,2,2,8,1024]{4,3,1,2,0:T(8,128)}), f32[16,2,2,8,1024]{4,3,1,2,0:T(8,128)}, u32[]{:S(2)}, u32[]{:S(2)}) async-start(f32[16,2,2,8,1024]{4,3,1,2,0:T(8,128)} %bitcast.489), calls=%async_computation.1 | async-start | bytes 4194304 | tf_op jit(solution)/shard_map/all_to_all | solution.py:39
  283.4 2.7 fusion.34
  287.1 6.3 %subtract_convert_fusion.1 = (bf16[1024,3,1,512]{3,0,2,1:T(8,128)(2,1)}, bf16[1024,3,1,512]{3,0,2,1:T(8,128)(2,1)}) fusion(f32[1024,512]{1,0:T(8,128)S(1)} %get-tuple-element.66, f32[3,512]{1,0:T(4,128)S(1)} %copy-done.18, f32[1024,512]{1,0:T(8,128)S(1)} %get-tuple-element.63, f32[3,512]{1,0:T(4,128)S(1)} %copy-done.27, ...), kind=kLoop, calls=%fused_computation.31 | loop fusion | flops 37748736 | bytes 18911232 | tf_op jit(solution)/shard_map/convert_element_type | solution.py:92
  293.4 59.5 %all-to-all-done.1 = f32[16,2,2,8,1024]{4,3,1,2,0:T(8,128)} async-done(((f32[16,2,2,8,1024]{4,3,1,2,0:T(8,128)}), f32[16,2,2,8,1024]{4,3,1,2,0:T(8,128)}, u32[]{:S(2)}, u32[]{:S(2)}) %all-to-all-start.1) | async-done | bytes 2097184 | tf_op jit(solution)/shard_map/all_to_all | solution.py:39
  352.9 6.1 %all-to-all-start.3 = ((f32[16,2,2,8,1024]{4,3,1,2,0:T(8,128)}), f32[16,2,2,8,1024]{4,3,1,2,0:T(8,128)}, u32[]{:S(2)}, u32[]{:S(2)}) async-start(f32[16,2,2,8,1024]{4,3,1,2,0:T(8,128)} %bitcast.450), calls=%async_computation.3 | async-start | bytes 4194304 | tf_op jit(solution)/shard_map/all_to_all | solution.py:39
  359.0 7.3 %fusion.19 = f32[2,2,16,8,1024]{4,3,2,0,1:T(8,128)S(1)} fusion(bf16[1024,3,1,512]{3,0,2,1:T(8,128)(2,1)} %get-tuple-element.15, bf16[1024,3,1,512]{3,0,2,1:T(8,128)(2,1)} %get-tuple-element.14, bf16[1,2,128,3,2,512]{5,2,4,3,1,0:T(8,128)(2,1)} %get-tuple-element.95, bf16[1,2,128,3,2,512]{5,2,4,3,1,0:T(8,128)(2,1)} %get-tuple-element.94), kind=kOutput, calls=%fused_computation.60 | convolution fusion | flops 3240099840 | bytes 11534336 | tf_op jit(solution)/shard_map/qpicrs,jcrs->pqij/dot_general | solution.py:130
  367.8 3.9 constant_dynamic-update-slice_fusion.3
  371.7 6.1 %constant_dynamic-update-slice_fusion.2 = (bf16[1024,3,2,768]{3,0,2,1:T(8,128)(2,1)}, bf16[1024,3,2,768]{3,0,2,1:T(8,128)(2,1)}) fusion(bf16[1024,3,2,768]{3,0,2,1:T(8,128)(2,1)} %constant_dynamic-update-slice_fusion.3, bf16[1024,3,2,512]{3,0,2,1:T(8,128)(2,1)S(1)} %bitcast.483), kind=kLoop, calls=%fused_computation.169 | loop fusion | bytes 18874368 | tf_op jit(solution)/shard_map/concatenate | solution.py:21
  377.8 3.9 constant_dynamic-update-slice_fusion
  381.7 3.7 slice_bitcast_fusion.7
  385.5 5.1 fusion.46
  390.5 7.4 %all-to-all-start.4 = ((f32[16,2,2,8,1024]{4,3,1,2,0:T(8,128)}), f32[16,2,2,8,1024]{4,3,1,2,0:T(8,128)S(1)}, u32[]{:S(2)}, u32[]{:S(2)}) async-start(f32[16,2,2,8,1024]{4,3,1,2,0:T(8,128)} %bitcast.490), calls=%async_computation.4 | async-start | bytes 4194304 | tf_op jit(solution)/shard_map/all_to_all | solution.py:39
  398.0 8.4 %subtract_convert_fusion.3 = (bf16[1024,3,1,512]{3,0,2,1:T(8,128)(2,1)S(1)}, bf16[1024,3,1,512]{3,0,2,1:T(8,128)(2,1)S(1)}) fusion(f32[1024,512]{1,0:T(8,128)} %get-tuple-element.78, f32[3,512]{1,0:T(4,128)S(1)} %bitcast.507, f32[1024,512]{1,0:T(8,128)} %get-tuple-element.160, f32[3,512]{1,0:T(4,128)S(1)} %bitcast.508, f32[1024,512]{1,0:T(8,128)} %get-tuple-element.79, ...), kind=kLoop, calls=%fused_computation.35 | loop fusion | flops 37748736 | bytes 18911232 | tf_op jit(solution)/shard_map/convert_element_type | solution.py:92
  406.5 3.4 fusion.21
  412.0 5.1 %fusion.28 = (f32[1024,512]{1,0:T(8,128)}, f32[1024,512]{1,0:T(8,128)}, f32[1024,512]{1,0:T(8,128)}, f32[1024,512]{1,0:T(8,128)}, f32[1024,512]{1,0:T(8,128)}, /*index=5*/f32[1024,512]{1,0:T(8,128)}) fusion(bf16[1024,3,512]{2,0,1:T(8,128)(2,1)S(1)} %get-tuple-element.25, bf16[1024,3,512]{2,0,1:T(8,128)(2,1)S(1)} %get-tuple-element.24), kind=kLoop, calls=%fused_computation.79 | loop fusion | flops 3145728 | bytes 18874368 | tf_op jit(solution)/shard_map/mul | solution.py:51
  417.1 10.0 %all-to-all-done.4 = f32[16,2,2,8,1024]{4,3,1,2,0:T(8,128)S(1)} async-done(((f32[16,2,2,8,1024]{4,3,1,2,0:T(8,128)}), f32[16,2,2,8,1024]{4,3,1,2,0:T(8,128)S(1)}, u32[]{:S(2)}, u32[]{:S(2)}) %all-to-all-start.4) | async-done | bytes 2097184 | tf_op jit(solution)/shard_map/all_to_all | solution.py:39
  427.1 5.0 all-to-all-start.2
  432.1 7.8 %subtract_convert_fusion = (bf16[1024,3,1,512]{3,0,2,1:T(8,128)(2,1)S(1)}, bf16[1024,3,1,512]{3,0,2,1:T(8,128)(2,1)S(1)}) fusion(f32[1024,512]{1,0:T(8,128)} %get-tuple-element.60, f32[3,512]{1,0:T(4,128)S(1)} %copy-done.21, f32[1024,512]{1,0:T(8,128)} %get-tuple-element.167, f32[3,512]{1,0:T(4,128)S(1)} %copy-done.24, f32[1024,512]{1,0:T(8,128)} %get-tuple-element.61, ...), kind=kLoop, calls=%fused_computation.29 | loop fusion | flops 37748736 | bytes 18911232 | tf_op jit(solution)/shard_map/convert_element_type | solution.py:92
  440.0 3.4 fusion.18
  444.9 16.4 %all-to-all-done.2 = f32[16,2,2,8,1024]{4,3,1,2,0:T(8,128)} async-done(((f32[16,2,2,8,1024]{4,3,1,2,0:T(8,128)}), f32[16,2,2,8,1024]{4,3,1,2,0:T(8,128)}, u32[]{:S(2)}, u32[]{:S(2)}) %all-to-all-start.2) | async-done | bytes 2097184 | tf_op jit(solution)/shard_map/all_to_all | solution.py:39
  461.3 5.0 all-to-all-start.5
  474.0 21.5 %all-to-all-done.5 = f32[16,2,2,8,1024]{4,3,1,2,0:T(8,128)} async-done(((f32[16,2,2,8,1024]{4,3,1,2,0:T(8,128)}), f32[16,2,2,8,1024]{4,3,1,2,0:T(8,128)}, u32[]{:S(2)}, u32[]{:S(2)}) %all-to-all-start.5) | async-done | bytes 2097184 | tf_op jit(solution)/shard_map/all_to_all | solution.py:39
  (186 shorter events, 37.9 us)
Async XLA Ops:
  6.5 135.2 %all-gather.2.cloned.1.call-start = ((), (), s32[]{:S(2)}) async-start(), calls=%async_computation.6 | async-start | bytes 7077888 | tf_op jit(solution)/shard_map/all_gather | solution.py:105
  9.6 6.8 %collective-permute-start.1 = (f32[3,3,2,256]{3,2,1,0:T(2,128)S(1)}, f32[3,3,2,256]{3,2,1,0:T(2,128)S(1)}, u32[]{:S(2)}, u32[]{:S(2)}) collective-permute-start(f32[3,3,2,256]{3,2,1,0:T(2,128)S(1)} %slice_bitcast_fusion.53), channel_id=1, source_target_pairs={{0,1},{1,2},{2,3},{3,4},{4,5},{5,6},{6,7},{7,8},{8,9},{9,10},{10,1... | collective-permute-start | bytes 55304 | tf_op jit(solution)/shard_map/ppermute | solution.py:13
  141.8 7.9 %copy-start = (bf16[1024,3,2,512]{3,0,2,1:T(8,128)(2,1)S(1)}, bf16[1024,3,2,512]{3,0,2,1:T(8,128)(2,1)}, u32[]{:S(2)}) copy-start(bf16[1024,3,2,512]{3,0,2,1:T(8,128)(2,1)} %all-gather.2.cloned.1.call-done) | copy-start | bytes 18874372
  181.6 5.0 copy-start.2
  181.6 5.0 copy-start.7
  191.5 16.7 %slice-start = ((s8[6291456]{0:T(1024)(128)(4,1)}), s8[2097152]{0:T(1024)(128)(4,1)S(1)}, s32[]{:S(2)}) async-start(s8[6291456]{0:T(1024)(128)(4,1)} %bitcast.480), calls=%async_computation.7 | async-start | bytes 4194304
  191.5 86.4 %all-to-all-start = ((f32[16,2,2,8,1024]{4,3,1,2,0:T(8,128)}), f32[16,2,2,8,1024]{4,3,1,2,0:T(8,128)}, u32[]{:S(2)}, u32[]{:S(2)}) async-start(f32[16,2,2,8,1024]{4,3,1,2,0:T(8,128)} %bitcast.488), calls=%async_computation | async-start | bytes 4194304 | tf_op jit(solution)/shard_map/all_to_all | solution.py:39
  198.0 10.3 %slice-start.1 = ((s8[6291456]{0:T(1024)(128)(4,1)}), s8[4194304]{0:T(1024)(128)(4,1)S(1)}, s32[]{:S(2)}) async-start(s8[6291456]{0:T(1024)(128)(4,1)} %bitcast.480), calls=%async_computation.8 | async-start | bytes 8388608
  242.5 5.4 %copy-start.3 = (bf16[1,2,128,3,2,512]{5,2,4,3,1,0:T(8,128)(2,1)S(1)}, bf16[1,2,128,3,2,512]{5,2,4,3,1,0:T(8,128)(2,1)}, u32[]{:S(2)}) copy-start(bf16[1,2,128,3,2,512]{5,2,4,3,1,0:T(8,128)(2,1)} %get-tuple-element.94) | copy-start | bytes 4718596
  252.7 10.2 %slice-start.4 = ((s8[6291456]{0:T(1024)(128)(4,1)}), s8[4194304]{0:T(1024)(128)(4,1)S(1)}, s32[]{:S(2)}) async-start(s8[6291456]{0:T(1024)(128)(4,1)} %bitcast.484), calls=%async_computation.11 | async-start | bytes 8388608
  254.3 8.6 %slice-start.5 = ((s8[6291456]{0:T(1024)(128)(4,1)}), s8[2097152]{0:T(1024)(128)(4,1)S(1)}, s32[]{:S(2)}) async-start(s8[6291456]{0:T(1024)(128)(4,1)} %bitcast.484), calls=%async_computation.12 | async-start | bytes 4194304
  257.5 110.3 %collective-permute-start.2 = (bf16[1024,3,2,256]{3,0,2,1:T(8,128)(2,1)}, bf16[1024,3,2,256]{3,0,2,1:T(8,128)(2,1)}, u32[]{:S(2)}, u32[]{:S(2)}) collective-permute-start(bf16[1024,3,2,256]{3,0,2,1:T(8,128)(2,1)} %get-tuple-element.30), channel_id=1, source_target_pairs={{0,1},{1,2},{2,3},{3,4},{4,5},{5,6},{6,7},{7,8},{8,9},{9,10},{10,1... | collective-permute-start | bytes 9437192 | tf_op jit(solution)/shard_map/ppermute | solution.py:23
  258.0 119.8 %collective-permute-start = (bf16[1024,3,2,256]{3,0,2,1:T(8,128)(2,1)}, bf16[1024,3,2,256]{3,0,2,1:T(8,128)(2,1)}, u32[]{:S(2)}, u32[]{:S(2)}) collective-permute-start(bf16[1024,3,2,256]{3,0,2,1:T(8,128)(2,1)} %get-tuple-element.31), channel_id=1, source_target_pairs={{1,0},{2,1},{3,2},{4,3},{5,4},{6,5},{7,6},{8,7},{9,8},{10,9},{11,1... | collective-permute-start | bytes 9437192 | tf_op jit(solution)/shard_map/ppermute | solution.py:25
  265.9 2.1 copy-start.1
  268.1 4.9 copy-start.4
  268.1 4.9 copy-start.8
  277.9 75.0 %all-to-all-start.1 = ((f32[16,2,2,8,1024]{4,3,1,2,0:T(8,128)}), f32[16,2,2,8,1024]{4,3,1,2,0:T(8,128)}, u32[]{:S(2)}, u32[]{:S(2)}) async-start(f32[16,2,2,8,1024]{4,3,1,2,0:T(8,128)} %bitcast.489), calls=%async_computation.1 | async-start | bytes 4194304 | tf_op jit(solution)/shard_map/all_to_all | solution.py:39
  286.1 0.9 copy-start.17
  286.1 0.9 copy-start.18
  286.1 0.9 copy-start.19
  286.1 0.9 copy-start.26
  286.1 0.9 copy-start.27
  352.9 37.6 %all-to-all-start.3 = ((f32[16,2,2,8,1024]{4,3,1,2,0:T(8,128)}), f32[16,2,2,8,1024]{4,3,1,2,0:T(8,128)}, u32[]{:S(2)}, u32[]{:S(2)}) async-start(f32[16,2,2,8,1024]{4,3,1,2,0:T(8,128)} %bitcast.450), calls=%async_computation.3 | async-start | bytes 4194304 | tf_op jit(solution)/shard_map/all_to_all | solution.py:39
  359.0 12.7 %slice-start.2 = ((s8[6291456]{0:T(1024)(128)(4,1)}), s8[4194304]{0:T(1024)(128)(4,1)S(1)}, s32[]{:S(2)}) async-start(s8[6291456]{0:T(1024)(128)(4,1)} %bitcast.482), calls=%async_computation.9 | async-start | bytes 8388608
  359.0 12.7 %slice-start.3 = ((s8[6291456]{0:T(1024)(128)(4,1)}), s8[2097152]{0:T(1024)(128)(4,1)S(1)}, s32[]{:S(2)}) async-start(s8[6291456]{0:T(1024)(128)(4,1)} %bitcast.482), calls=%async_computation.10 | async-start | bytes 4194304
  385.4 12.5 %copy-start.11 = (f32[3,1,512]{2,0,1:T(4,128)S(1)}, f32[3,1,512]{2,0,1:T(4,128)}, u32[]{:S(2)}) copy-start(f32[3,1,512]{2,0,1:T(4,128)} %copy.137) | copy-start | bytes 18436
  385.4 12.5 %copy-start.12 = (f32[3,1,512]{2,0,1:T(4,128)S(1)}, f32[3,1,512]{2,0,1:T(4,128)}, u32[]{:S(2)}) copy-start(f32[3,1,512]{2,0,1:T(4,128)} %copy.138) | copy-start | bytes 18436
  385.4 12.5 %copy-start.13 = (f32[3,1,512]{2,0,1:T(4,128)S(1)}, f32[3,1,512]{2,0,1:T(4,128)}, u32[]{:S(2)}) copy-start(f32[3,1,512]{2,0,1:T(4,128)} %copy.139) | copy-start | bytes 18436
  385.4 12.5 %copy-start.14 = (f32[3,1,512]{2,0,1:T(4,128)S(1)}, f32[3,1,512]{2,0,1:T(4,128)}, u32[]{:S(2)}) copy-start(f32[3,1,512]{2,0,1:T(4,128)} %copy.140) | copy-start | bytes 18436
  385.4 12.5 %copy-start.15 = (f32[3,1,512]{2,0,1:T(4,128)S(1)}, f32[3,1,512]{2,0,1:T(4,128)}, u32[]{:S(2)}) copy-start(f32[3,1,512]{2,0,1:T(4,128)} %copy.141) | copy-start | bytes 18436
  385.4 12.5 %copy-start.16 = (f32[3,1,512]{2,0,1:T(4,128)S(1)}, f32[3,1,512]{2,0,1:T(4,128)}, u32[]{:S(2)}) copy-start(f32[3,1,512]{2,0,1:T(4,128)} %copy.142) | copy-start | bytes 18436
  390.5 36.5 %all-to-all-start.4 = ((f32[16,2,2,8,1024]{4,3,1,2,0:T(8,128)}), f32[16,2,2,8,1024]{4,3,1,2,0:T(8,128)S(1)}, u32[]{:S(2)}, u32[]{:S(2)}) async-start(f32[16,2,2,8,1024]{4,3,1,2,0:T(8,128)} %bitcast.490), calls=%async_computation.4 | async-start | bytes 4194304 | tf_op jit(solution)/shard_map/all_to_all | solution.py:39
  398.0 8.5 %copy-start.5 = (bf16[1,2,128,3,2,512]{5,2,4,3,1,0:T(8,128)(2,1)S(1)}, bf16[1,2,128,3,2,512]{5,2,4,3,1,0:T(8,128)(2,1)}, u32[]{:S(2)}) copy-start(bf16[1,2,128,3,2,512]{5,2,4,3,1,0:T(8,128)(2,1)} %get-tuple-element.94) | copy-start | bytes 4718596
  398.0 8.5 %copy-start.9 = (bf16[1,2,128,3,2,512]{5,2,4,3,1,0:T(8,128)(2,1)S(1)}, bf16[1,2,128,3,2,512]{5,2,4,3,1,0:T(8,128)(2,1)}, u32[]{:S(2)}) copy-start(bf16[1,2,128,3,2,512]{5,2,4,3,1,0:T(8,128)(2,1)} %get-tuple-element.95) | copy-start | bytes 4718596
  398.0 13.4 %slice-start.6 = ((s8[9437184]{0:T(1024)(128)(4,1)}), s8[4194304]{0:T(1024)(128)(4,1)S(1)}, s32[]{:S(2)}) async-start(s8[9437184]{0:T(1024)(128)(4,1)} %bitcast.486), calls=%async_computation.13 | async-start | bytes 8388608
  406.4 4.9 slice-start.7
  406.5 4.9 slice-start.8
  411.9 20.1 %copy-start.20 = (f32[3,512]{1,0:T(4,128)S(1)}, f32[3,512]{1,0:T(4,128)}, u32[]{:S(2)}) copy-start(f32[3,512]{1,0:T(4,128)} %get-tuple-element.116) | copy-start | bytes 18436
  411.9 20.1 %copy-start.21 = (f32[3,512]{1,0:T(4,128)S(1)}, f32[3,512]{1,0:T(4,128)}, u32[]{:S(2)}) copy-start(f32[3,512]{1,0:T(4,128)} %get-tuple-element.117) | copy-start | bytes 18436
  411.9 20.1 %copy-start.22 = (f32[3,512]{1,0:T(4,128)S(1)}, f32[3,512]{1,0:T(4,128)}, u32[]{:S(2)}) copy-start(f32[3,512]{1,0:T(4,128)} %get-tuple-element.118) | copy-start | bytes 18436
  411.9 20.1 %copy-start.23 = (f32[3,512]{1,0:T(4,128)S(1)}, f32[3,512]{1,0:T(4,128)}, u32[]{:S(2)}) copy-start(f32[3,512]{1,0:T(4,128)} %get-tuple-element.113) | copy-start | bytes 18436
  411.9 20.1 %copy-start.24 = (f32[3,512]{1,0:T(4,128)S(1)}, f32[3,512]{1,0:T(4,128)}, u32[]{:S(2)}) copy-start(f32[3,512]{1,0:T(4,128)} %get-tuple-element.114) | copy-start | bytes 18436
  411.9 20.1 %copy-start.25 = (f32[3,512]{1,0:T(4,128)S(1)}, f32[3,512]{1,0:T(4,128)}, u32[]{:S(2)}) copy-start(f32[3,512]{1,0:T(4,128)} %get-tuple-element.115) | copy-start | bytes 18436
  427.1 34.2 %all-to-all-start.2 = ((f32[16,2,2,8,1024]{4,3,1,2,0:T(8,128)}), f32[16,2,2,8,1024]{4,3,1,2,0:T(8,128)}, u32[]{:S(2)}, u32[]{:S(2)}) async-start(f32[16,2,2,8,1024]{4,3,1,2,0:T(8,128)} %bitcast.491), calls=%async_computation.2 | async-start | bytes 4194304 | tf_op jit(solution)/shard_map/all_to_all | solution.py:39
  432.1 7.8 %copy-start.6 = (bf16[1,2,128,3,2,512]{5,2,4,3,1,0:T(8,128)(2,1)S(1)}, bf16[1,2,128,3,2,512]{5,2,4,3,1,0:T(8,128)(2,1)}, u32[]{:S(2)}) copy-start(bf16[1,2,128,3,2,512]{5,2,4,3,1,0:T(8,128)(2,1)} %get-tuple-element.94) | copy-start | bytes 4718596
  432.1 7.8 %copy-start.10 = (bf16[1,2,128,3,2,512]{5,2,4,3,1,0:T(8,128)(2,1)S(1)}, bf16[1,2,128,3,2,512]{5,2,4,3,1,0:T(8,128)(2,1)}, u32[]{:S(2)}) copy-start(bf16[1,2,128,3,2,512]{5,2,4,3,1,0:T(8,128)(2,1)} %get-tuple-element.95) | copy-start | bytes 4718596
  461.3 34.2 %all-to-all-start.5 = ((f32[16,2,2,8,1024]{4,3,1,2,0:T(8,128)}), f32[16,2,2,8,1024]{4,3,1,2,0:T(8,128)}, u32[]{:S(2)}, u32[]{:S(2)}) async-start(f32[16,2,2,8,1024]{4,3,1,2,0:T(8,128)} %bitcast.492), calls=%async_computation.5 | async-start | bytes 4194304 | tf_op jit(solution)/shard_map/all_to_all | solution.py:39
  469.8 28.8 %copy-start.29 = (s32[6]{0:T(128)S(1)}, s32[6]{0:T(128)}, u32[]{:S(2)}) copy-start(s32[6]{0:T(128)} %param.6) | copy-start | bytes 76
  (1 other events, 0.9 us)
Sparse Core Ops, SparseCore 0:
  9.0 132.7 all-gather.1
where the time goes:
time: 511 us; the launch traced here: 508 us
  waiting for transfers between devices  228 us (45%)
  other arithmetic  106 us (21%)
  local copies, waits for them, and re-layouts  91.6 us (18%)
  starting transfers between devices  40.7 us (8%)
  matrix products  26.5 us (5%)
  between operations  14.8 us (3%)
    all_gather x1, waiting for transfers between devices, on_device(): gathered = lax.all_gather(vectors, 'vec', axis=0, tiled=True)  120 us
    all_to_all x6, waiting for transfers between devices, sum_at_owner(): lax.all_to_all(blocks, axis, split_axis=0, concat_axis=0, tiled=True)  107 us
    convert_element_type x6, other arithmetic, displace(): disp_real.astype(jnp.bfloat16)  37.8 us
    all_to_all x6, starting transfers between devices, sum_at_owner(): lax.all_to_all(blocks, axis, split_axis=0, concat_axis=0, tiled=True)  35.3 us
    select_n x2, other arithmetic, neighbour(): return jnp.where(position == extent - 1, beside_all, inside)  34.9 us
    dot_general x6, matrix products, on_device(): jnp.einsum('qpicrs,jcrs->pqij', left_side, displaced, preferred_element_t...  25.9 us
    slice x8, local copies, waits for them, and re-layouts, neighbour(): beside_all = jnp.roll(field, -(extent - 1) * stride, axis=-1)  24.6 us
    mul x10, other arithmetic, colour_apply(): out_real = out_real + left_real * right_real - left_imag * right_imag  19 us
  transfers between devices with their start and end apart: 10, of which 5 were waited for; matrix products, arithmetic and copies ran while one was open for 33% of the time, Pallas kernels for 0%

commit v1 on v0

--- a/solution.py
+++ b/solution.py
@@ -102,7 +102,10 @@
     y_index = flat // LX % LY
     z_index = lax.axis_index("gz") * depth + flat // plane
     lower_links = from_behind(links[2, :, :, :, sites - plane :], "gz", 1)
-    gathered = lax.all_gather(vectors, "vec", axis=0, tiled=True)
+    size = lax.axis_size("vec")
+    pieces = jnp.stack([vectors for _ in range(size)])
+    pieces = lax.all_to_all(pieces, "vec", split_axis=0, concat_axis=0)
+    gathered = jnp.concatenate(pieces, axis=0)
     extended = extended_2(gathered, (("gz", 3),), plane)
     momenta = moms.astype(jnp.float32)
     theta = (

time: 511 us -> 453 us (0.89)
  the two profiles are of different devices: /device:TPU:40 before, /device:TPU:1 now
where the time goes in v1:
time: 453 us; the launch traced here: 449 us
  waiting for transfers between devices  184 us (41%)
  other arithmetic  113 us (25%)
  local copies, waits for them, and re-layouts  72 us (16%)
  starting transfers between devices  53.9 us (12%)
  matrix products  25.1 us (6%)
    all_to_all x6, waiting for transfers between devices, sum_at_owner(): lax.all_to_all(blocks, axis, split_axis=0, concat_axis=0, tiled=True)  112 us
    ppermute x1, waiting for transfers between devices, from_behind(): lax.ppermute(shard, axis, [(i, (i + by) % peers) for i in range(peers)])  40.7 us
    all_to_all x6, starting transfers between devices, sum_at_owner(): lax.all_to_all(blocks, axis, split_axis=0, concat_axis=0, tiled=True)  40.1 us
    convert_element_type x6, other arithmetic, displace(): disp_real.astype(jnp.bfloat16)  40 us
    select_n x2, other arithmetic, neighbour(): return jnp.where(position == extent - 1, beside_all, inside)  35.1 us
    all_to_all x1, waiting for transfers between devices, on_device(): pieces = lax.all_to_all(pieces, 'vec', split_axis=0, concat_axis=0)  31.4 us
    dot_general x6, matrix products, on_device(): jnp.einsum('qpicrs,jcrs->pqij', left_side, displaced, preferred_element_t...  24.5 us
    mul x10, other arithmetic, colour_apply(): out_real = out_real + left_real * right_real - left_imag * right_imag  21 us
  transfers between devices with their start and end apart: 10, of which 7 were waited for; matrix products, arithmetic and copies ran while one was open for 28% of the time, Pallas kernels for 0%

profile of v1, /device:TPU:1, one launch (start us, length us, event | category | flops | bytes accessed | tf_op | source)
XLA Modules:
  0.0 449.1 jit_solution(8223257192149292229)
XLA Ops:
  1.2 3.5 stack.38
  4.7 6.5 %all-to-all-start = ((bf16[8,128,3,2,512]{4,1,2,3,0:T(8,128)(2,1)}), bf16[8,128,3,2,512]{4,1,2,3,0:T(8,128)(2,1)}, u32[]{:S(2)}, u32[]{:S(2)}) async-start(bf16[8,128,3,2,512]{4,1,2,3,0:T(8,128)(2,1)} %stack.38), calls=%async_computation | async-start | bytes 12582912 | tf_op jit(solution)/shard_map/all_to_all | solution.py:107
  11.2 4.2 collective-permute-start.1
  17.3 1.9 maximum_bitcast_fusion.26
  21.0 40.7 %collective-permute-done.1 = f32[3,3,2,256]{3,2,1,0:T(2,128)S(1)} collective-permute-done((f32[3,3,2,256]{3,2,1,0:T(2,128)S(1)}, f32[3,3,2,256]{3,2,1,0:T(2,128)S(1)}, u32[]{:S(2)}, u32[]{:S(2)}) %collective-permute-start.1) | collective-permute-done | bytes 18464 | tf_op jit(solution)/shard_map/ppermute | solution.py:13
  66.8 31.4 %all-to-all-done = bf16[8,128,3,2,512]{4,1,2,3,0:T(8,128)(2,1)} async-done(((bf16[8,128,3,2,512]{4,1,2,3,0:T(8,128)(2,1)}), bf16[8,128,3,2,512]{4,1,2,3,0:T(8,128)(2,1)}, u32[]{:S(2)}, u32[]{:S(2)}) %all-to-all-start) | async-done | bytes 6291488 | tf_op jit(solution)/shard_map/all_to_all | solution.py:107
  98.3 3.2 copy.34
  101.5 7.1 %fusion.94 = (bf16[1024,3,2,481]{3,0,2,1:T(8,128)(2,1)}, bf16[1024,3,2,481]{3,0,2,1:T(8,128)(2,1)}) fusion(bf16[1024,3,2,512]{3,0,2,1:T(8,128)(2,1)S(1)} %bitcast.481), kind=kLoop, calls=%fused_computation.254 | loop fusion | bytes 23642112 | tf_op jit(solution)/shard_map/jit(_roll_static)/slice | solution.py:62
  108.6 2.4 fusion.95
  111.0 2.4 fusion.92
  113.4 6.3 %fusion.93 = (bf16[1024,3,2,511]{3,0,2,1:T(8,128)(2,1)}, bf16[1024,3,2,511]{3,0,2,1:T(8,128)(2,1)}) fusion(bf16[1024,3,2,512]{3,0,2,1:T(8,128)(2,1)S(1)} %bitcast.484), kind=kLoop, calls=%fused_computation.253 | loop fusion | bytes 25116672 | tf_op jit(solution)/shard_map/jit(_roll_static)/slice | solution.py:61
  119.7 6.8 %fusion.90 = (bf16[1024,3,2,288]{3,0,2,1:T(8,128)(2,1)}, bf16[1024,3,2,288]{3,0,2,1:T(8,128)(2,1)}) fusion(bf16[1024,3,2,512]{3,0,2,1:T(8,128)(2,1)S(1)} %bitcast.485), kind=kLoop, calls=%fused_computation.250 | loop fusion | bytes 14155776 | tf_op jit(solution)/shard_map/jit(_roll_static)/slice | solution.py:62
  126.5 3.7 fusion.91
  130.2 2.4 fusion.88
  132.6 6.5 %fusion.89 = (bf16[1024,3,2,480]{3,0,2,1:T(8,128)(2,1)}, bf16[1024,3,2,480]{3,0,2,1:T(8,128)(2,1)}) fusion(bf16[1024,3,2,512]{3,0,2,1:T(8,128)(2,1)S(1)} %bitcast.488), kind=kLoop, calls=%fused_computation.249 | loop fusion | bytes 23592960 | tf_op jit(solution)/shard_map/jit(_roll_static)/slice | solution.py:61
  139.1 3.2 fusion.87
  142.3 18.0 %maximum_select_fusion = (bf16[1024,3,2,512]{3,0,2,1:T(8,128)(2,1)S(1)}, bf16[1024,3,2,512]{3,0,2,1:T(8,128)(2,1)}) fusion(bf16[1024,3,2,481]{3,0,2,1:T(8,128)(2,1)} %get-tuple-element.49, bf16[1024,3,2,31]{3,0,2,1:T(8,128)(2,1)} %get-tuple-element.51, bf16[1024,3,2,1]{3,0,2,1:T(8,128)(2,1)} %get-tuple-element.45, ...), kind=kLoop, calls=%fused_computation | loop fusion | flops 56623104 | bytes 37749760 | tf_op jit(solution)/shard_map/jit(_where)/select_n | solution.py:60
  162.8 4.9 %subtract_convert_fusion.5 = (bf16[1024,3,1,512]{3,0,2,1:T(8,128)(2,1)S(1)}, bf16[1024,3,1,512]{3,0,2,1:T(8,128)(2,1)S(1)}) fusion(f32[1024,512]{1,0:T(8,128)S(1)} %get-tuple-element.90, f32[3,512]{1,0:T(4,128)S(1)} %bitcast.530, f32[1024,512]{1,0:T(8,128)S(1)} %get-tuple-element.87, f32[3,512]{1,0:T(4,128)S(1)} %bitcast.531, ...), kind=kLoop, calls=%fused_computation.39 | loop fusion | flops 37748736 | bytes 18911232 | tf_op jit(solution)/shard_map/convert_element_type | solution.py:92
  167.7 3.4 fusion.25
  172.6 9.7 %all-to-all-start.1 = ((f32[16,2,2,8,1024]{4,3,1,2,0:T(8,128)}), f32[16,2,2,8,1024]{4,3,1,2,0:T(8,128)}, u32[]{:S(2)}, u32[]{:S(2)}) async-start(f32[16,2,2,8,1024]{4,3,1,2,0:T(8,128)} %bitcast.499), calls=%async_computation.1 | async-start | bytes 4194304 | tf_op jit(solution)/shard_map/all_to_all | solution.py:39
  182.3 17.1 %maximum_select_fusion.1 = (bf16[1024,3,2,512]{3,0,2,1:T(8,128)(2,1)S(1)}, bf16[1024,3,2,512]{3,0,2,1:T(8,128)(2,1)}) fusion(bf16[1024,3,2,288]{3,0,2,1:T(8,128)(2,1)} %get-tuple-element.39, bf16[1024,3,2,224]{3,0,2,1:T(8,128)(2,1)} %get-tuple-element.41, bf16[1024,3,2,32]{3,0,2,1:T(8,128)(2,1)} %get-tuple-element.35, ...), kind=kLoop, calls=%fused_computation.5 | loop fusion | flops 56623104 | bytes 37749760 | tf_op jit(solution)/shard_map/jit(_where)/select_n | solution.py:60
  201.3 4.9 %subtract_convert_fusion.4 = (bf16[1024,3,1,512]{3,0,2,1:T(8,128)(2,1)S(1)}, bf16[1024,3,1,512]{3,0,2,1:T(8,128)(2,1)S(1)}) fusion(f32[1024,512]{1,0:T(8,128)S(1)} %get-tuple-element.84, f32[3,512]{1,0:T(4,128)S(1)} %bitcast.524, f32[1024,512]{1,0:T(8,128)S(1)} %get-tuple-element.81, f32[3,512]{1,0:T(4,128)S(1)} %bitcast.525, ...), kind=kLoop, calls=%fused_computation.37 | loop fusion | flops 37748736 | bytes 18911232 | tf_op jit(solution)/shard_map/convert_element_type | solution.py:92
  206.3 3.4 fusion.24
  211.2 3.1 collective-permute-start.2
  216.9 6.5 %subtract_convert_fusion.2 = (bf16[1024,3,1,512]{3,0,2,1:T(8,128)(2,1)}, bf16[1024,3,1,512]{3,0,2,1:T(8,128)(2,1)}) fusion(f32[1024,512]{1,0:T(8,128)S(1)} %get-tuple-element.72, f32[3,512]{1,0:T(4,128)S(1)} %get-tuple-element.127, f32[1024,512]{1,0:T(8,128)S(1)} %get-tuple-element.69, f32[3,512]{1,0:T(4,128)S(1)} %get-tuple-element.124, ...), kind=kLoop, calls=%fused_computation.33 | loop fusion | flops 37748736 | bytes 18911232 | tf_op jit(solution)/shard_map/convert_element_type | solution.py:92
  223.5 7.5 %all-to-all-start.2 = ((f32[16,2,2,8,1024]{4,3,1,2,0:T(8,128)}), f32[16,2,2,8,1024]{4,3,1,2,0:T(8,128)}, u32[]{:S(2)}, u32[]{:S(2)}) async-start(f32[16,2,2,8,1024]{4,3,1,2,0:T(8,128)} %bitcast.500), calls=%async_computation.2 | async-start | bytes 4194304 | tf_op jit(solution)/shard_map/all_to_all | solution.py:39
  230.9 7.3 %fusion.22 = f32[2,2,16,8,1024]{4,3,2,0,1:T(8,128)S(1)} fusion(bf16[1024,3,1,512]{3,0,2,1:T(8,128)(2,1)} %get-tuple-element.17, bf16[1024,3,1,512]{3,0,2,1:T(8,128)(2,1)} %get-tuple-element.16, bf16[1,2,128,3,2,512]{5,2,4,3,1,0:T(8,128)(2,1)} %get-tuple-element.95, bf16[1,2,128,3,2,512]{5,2,4,3,1,0:T(8,128)(2,1)} %get-tuple-element.94), kind=kOutput, calls=%fused_computation.63 | convolution fusion | flops 3240099840 | bytes 11534336 | tf_op jit(solution)/shard_map/qpicrs,jcrs->pqij/dot_general | solution.py:133
  240.6 2.9 fusion.36
  243.6 2.9 fusion.37
  246.4 60.9 %all-to-all-done.2 = f32[16,2,2,8,1024]{4,3,1,2,0:T(8,128)} async-done(((f32[16,2,2,8,1024]{4,3,1,2,0:T(8,128)}), f32[16,2,2,8,1024]{4,3,1,2,0:T(8,128)}, u32[]{:S(2)}, u32[]{:S(2)}) %all-to-all-start.2) | async-done | bytes 2097184 | tf_op jit(solution)/shard_map/all_to_all | solution.py:39
  307.3 5.2 %all-to-all-start.4 = ((f32[16,2,2,8,1024]{4,3,1,2,0:T(8,128)}), f32[16,2,2,8,1024]{4,3,1,2,0:T(8,128)}, u32[]{:S(2)}, u32[]{:S(2)}) async-start(f32[16,2,2,8,1024]{4,3,1,2,0:T(8,128)} %bitcast.451), calls=%async_computation.4 | async-start | bytes 4194304 | tf_op jit(solution)/shard_map/all_to_all | solution.py:39
  312.6 8.0 %subtract_convert_fusion.1 = (bf16[1024,3,1,512]{3,0,2,1:T(8,128)(2,1)S(1)}, bf16[1024,3,1,512]{3,0,2,1:T(8,128)(2,1)S(1)}) fusion(f32[1024,512]{1,0:T(8,128)} %get-tuple-element.66, f32[3,512]{1,0:T(4,128)S(1)} %copy-done.21, f32[1024,512]{1,0:T(8,128)} %get-tuple-element.63, f32[3,512]{1,0:T(4,128)S(1)} %copy-done.24, f32[1024,512]{1,0:T(8,128)} %get-tuple-element.67, ...), kind=kLoop, calls=%fused_computation.31 | loop fusion | flops 37748736 | bytes 18911232 | tf_op jit(solution)/shard_map/convert_element_type | solution.py:92
  320.7 3.4 fusion.21
  325.6 4.5 %maximum_bitcast_fusion.12 = (bf16[1024,3,512]{2,0,1:T(8,128)(2,1)S(1)}, bf16[1024,3,512]{2,0,1:T(8,128)(2,1)}, bf16[1024,3,512]{2,0,1:T(8,128)(2,1)S(1)}, bf16[1024,3,512]{2,0,1:T(8,128)(2,1)S(1)}) fusion(bf16[1024,3,2,512]{3,0,2,1:T(8,128)(2,1)S(1)} %bitcast.492, bf16[1024,3,2,256]{3,0,2,1:T(8,128)(2,1)} %collective-permute-done.2, ...), kind=kLoop, calls=%fused_computation.42 | loop fusion | flops 25165824 | bytes 25165824 | tf_op jit(solution)/shard_map/squeeze | solution.py:91
  330.1 5.1 %fusion.48 = (f32[1024,512]{1,0:T(8,128)}, f32[1024,512]{1,0:T(8,128)}, f32[1024,512]{1,0:T(8,128)}, f32[1024,512]{1,0:T(8,128)}, f32[1024,512]{1,0:T(8,128)}, /*index=5*/f32[1024,512]{1,0:T(8,128)}) fusion(bf16[1024,3,512]{2,0,1:T(8,128)(2,1)S(1)} %get-tuple-element.28, bf16[1024,3,512]{2,0,1:T(8,128)(2,1)S(1)} %get-tuple-element.29), kind=kLoop, calls=%fused_computation.117 | loop fusion | flops 3145728 | bytes 18874368 | tf_op jit(solution)/shard_map/mul | solution.py:51
  335.2 5.8 %all-to-all-done.4 = f32[16,2,2,8,1024]{4,3,1,2,0:T(8,128)} async-done(((f32[16,2,2,8,1024]{4,3,1,2,0:T(8,128)}), f32[16,2,2,8,1024]{4,3,1,2,0:T(8,128)}, u32[]{:S(2)}, u32[]{:S(2)}) %all-to-all-start.4) | async-done | bytes 2097184 | tf_op jit(solution)/shard_map/all_to_all | solution.py:39
  341.0 6.2 %all-to-all-start.5 = ((f32[16,2,2,8,1024]{4,3,1,2,0:T(8,128)}), f32[16,2,2,8,1024]{4,3,1,2,0:T(8,128)}, u32[]{:S(2)}, u32[]{:S(2)}) async-start(f32[16,2,2,8,1024]{4,3,1,2,0:T(8,128)} %bitcast.501), calls=%async_computation.5 | async-start | bytes 4194304 | tf_op jit(solution)/shard_map/all_to_all | solution.py:39
  347.2 7.8 %subtract_convert_fusion.3 = (bf16[1024,3,1,512]{3,0,2,1:T(8,128)(2,1)S(1)}, bf16[1024,3,1,512]{3,0,2,1:T(8,128)(2,1)S(1)}) fusion(f32[1024,512]{1,0:T(8,128)} %get-tuple-element.78, f32[3,512]{1,0:T(4,128)S(1)} %bitcast.518, f32[1024,512]{1,0:T(8,128)} %get-tuple-element.161, f32[3,512]{1,0:T(4,128)S(1)} %bitcast.519, f32[1024,512]{1,0:T(8,128)} %get-tuple-element.79, ...), kind=kLoop, calls=%fused_computation.35 | loop fusion | flops 37748736 | bytes 18911232 | tf_op jit(solution)/shard_map/convert_element_type | solution.py:92
  355.1 3.4 fusion.23
  361.2 5.1 %fusion.30 = (f32[1024,512]{1,0:T(8,128)}, f32[1024,512]{1,0:T(8,128)}, f32[1024,512]{1,0:T(8,128)}, f32[1024,512]{1,0:T(8,128)}, f32[1024,512]{1,0:T(8,128)}, /*index=5*/f32[1024,512]{1,0:T(8,128)}) fusion(bf16[1024,3,512]{2,0,1:T(8,128)(2,1)S(1)} %copy-done.1, bf16[1024,3,512]{2,0,1:T(8,128)(2,1)S(1)} %get-tuple-element.24), kind=kLoop, calls=%fused_computation.81 | loop fusion | flops 3145728 | bytes 18874368 | tf_op jit(solution)/shard_map/mul | solution.py:51
  366.3 9.1 %all-to-all-done.5 = f32[16,2,2,8,1024]{4,3,1,2,0:T(8,128)} async-done(((f32[16,2,2,8,1024]{4,3,1,2,0:T(8,128)}), f32[16,2,2,8,1024]{4,3,1,2,0:T(8,128)}, u32[]{:S(2)}, u32[]{:S(2)}) %all-to-all-start.5) | async-done | bytes 2097184 | tf_op jit(solution)/shard_map/all_to_all | solution.py:39
  375.4 5.8 %all-to-all-start.3 = ((f32[16,2,2,8,1024]{4,3,1,2,0:T(8,128)}), f32[16,2,2,8,1024]{4,3,1,2,0:T(8,128)S(1)}, u32[]{:S(2)}, u32[]{:S(2)}) async-start(f32[16,2,2,8,1024]{4,3,1,2,0:T(8,128)} %bitcast.502), calls=%async_computation.3 | async-start | bytes 4194304 | tf_op jit(solution)/shard_map/all_to_all | solution.py:39
  381.3 7.8 %subtract_convert_fusion = (bf16[1024,3,1,512]{3,0,2,1:T(8,128)(2,1)S(1)}, bf16[1024,3,1,512]{3,0,2,1:T(8,128)(2,1)S(1)}) fusion(f32[1024,512]{1,0:T(8,128)} %get-tuple-element.60, f32[3,512]{1,0:T(4,128)S(1)} %copy-done.27, f32[1024,512]{1,0:T(8,128)} %get-tuple-element.158, f32[3,512]{1,0:T(4,128)S(1)} %copy-done.30, f32[1024,512]{1,0:T(8,128)} %get-tuple-element.61, ...), kind=kLoop, calls=%fused_computation.29 | loop fusion | flops 37748736 | bytes 18911232 | tf_op jit(solution)/shard_map/convert_element_type | solution.py:92
  389.1 3.4 fusion.20
  394.0 15.5 %all-to-all-done.3 = f32[16,2,2,8,1024]{4,3,1,2,0:T(8,128)S(1)} async-done(((f32[16,2,2,8,1024]{4,3,1,2,0:T(8,128)}), f32[16,2,2,8,1024]{4,3,1,2,0:T(8,128)S(1)}, u32[]{:S(2)}, u32[]{:S(2)}) %all-to-all-start.3) | async-done | bytes 2097184 | tf_op jit(solution)/shard_map/all_to_all | solution.py:39
  409.5 5.8 %all-to-all-start.6 = ((f32[16,2,2,8,1024]{4,3,1,2,0:T(8,128)}), f32[16,2,2,8,1024]{4,3,1,2,0:T(8,128)}, u32[]{:S(2)}, u32[]{:S(2)}) async-start(f32[16,2,2,8,1024]{4,3,1,2,0:T(8,128)} %bitcast.503), calls=%async_computation.6 | async-start | bytes 4194304 | tf_op jit(solution)/shard_map/all_to_all | solution.py:39
  417.2 1.7 reduce_sum.55
  423.0 20.7 %all-to-all-done.6 = f32[16,2,2,8,1024]{4,3,1,2,0:T(8,128)} async-done(((f32[16,2,2,8,1024]{4,3,1,2,0:T(8,128)}), f32[16,2,2,8,1024]{4,3,1,2,0:T(8,128)}, u32[]{:S(2)}, u32[]{:S(2)}) %all-to-all-start.6) | async-done | bytes 2097184 | tf_op jit(solution)/shard_map/all_to_all | solution.py:39
  (190 shorter events, 38.6 us)
Async XLA Ops:
  4.7 6.5 %copy-start.13 = (f32[3,3,3,2,512]{4,3,2,1,0:T(2,128)S(1)}, f32[3,3,3,2,512]{4,3,2,1,0:T(2,128)}, u32[]{:S(2)}) copy-start(f32[3,3,3,2,512]{4,3,2,1,0:T(2,128)} %param.5) | copy-start | bytes 331780
  4.7 10.7 %copy-start.2 = (bf16[128,3,2,512]{3,2,1,0:T(2,128)(2,1)S(1)}, bf16[128,3,2,512]{3,2,1,0:T(2,128)(2,1)}, u32[]{:S(2)}) copy-start(bf16[128,3,2,512]{3,2,1,0:T(2,128)(2,1)} %param.4) | copy-start | bytes 2359300
  4.7 11.2 %copy-start.32 = (s32[2,3]{1,0:T(2,128)S(1)}, s32[2,3]{1,0:T(2,128)}, u32[]{:S(2)}) copy-start(s32[2,3]{1,0:T(2,128)} %param.7) | copy-start | bytes 76
  4.7 93.6 %all-to-all-start = ((bf16[8,128,3,2,512]{4,1,2,3,0:T(8,128)(2,1)}), bf16[8,128,3,2,512]{4,1,2,3,0:T(8,128)(2,1)}, u32[]{:S(2)}, u32[]{:S(2)}) async-start(bf16[8,128,3,2,512]{4,1,2,3,0:T(8,128)(2,1)} %stack.38), calls=%async_computation | async-start | bytes 12582912 | tf_op jit(solution)/shard_map/all_to_all | solution.py:107
  11.2 50.5 %collective-permute-start.1 = (f32[3,3,2,256]{3,2,1,0:T(2,128)S(1)}, f32[3,3,2,256]{3,2,1,0:T(2,128)S(1)}, u32[]{:S(2)}, u32[]{:S(2)}) collective-permute-start(f32[3,3,2,256]{3,2,1,0:T(2,128)S(1)} %slice_bitcast_fusion.49), channel_id=1, source_target_pairs={{0,1},{1,2},{2,3},{3,4},{4,5},{5,6},{6,7},{7,8},{8,9},{9,10},{10,1... | collective-permute-start | bytes 55304 | tf_op jit(solution)/shard_map/ppermute | solution.py:13
  101.5 37.6 %copy-start = (bf16[8,128,3,2,512]{4,1,0,3,2:T(8,128)(2,1)}, bf16[8,128,3,2,512]{4,1,0,3,2:T(8,128)(2,1)S(1)}, u32[]{:S(2)}) copy-start(bf16[8,128,3,2,512]{4,1,0,3,2:T(8,128)(2,1)S(1)} %copy.34) | copy-start | bytes 18874372
  130.2 12.1 %slice-start.6 = ((s8[6291456]{0:T(1024)(128)(4,1)}), s8[4194304]{0:T(1024)(128)(4,1)S(1)}, s32[]{:S(2)}) async-start(s8[6291456]{0:T(1024)(128)(4,1)} %bitcast.497), calls=%async_computation.13 | async-start | bytes 8388608
  132.6 9.7 %slice-start.7 = ((s8[6291456]{0:T(1024)(128)(4,1)}), s8[2097152]{0:T(1024)(128)(4,1)S(1)}, s32[]{:S(2)}) async-start(s8[6291456]{0:T(1024)(128)(4,1)} %bitcast.497), calls=%async_computation.14 | async-start | bytes 4194304
  172.6 50.9 %all-to-all-start.1 = ((f32[16,2,2,8,1024]{4,3,1,2,0:T(8,128)}), f32[16,2,2,8,1024]{4,3,1,2,0:T(8,128)}, u32[]{:S(2)}, u32[]{:S(2)}) async-start(f32[16,2,2,8,1024]{4,3,1,2,0:T(8,128)} %bitcast.499), calls=%async_computation.1 | async-start | bytes 4194304 | tf_op jit(solution)/shard_map/all_to_all | solution.py:39
  201.3 5.0 %copy-start.4 = (bf16[1,2,128,3,2,512]{5,2,4,3,1,0:T(8,128)(2,1)S(1)}, bf16[1,2,128,3,2,512]{5,2,4,3,1,0:T(8,128)(2,1)}, u32[]{:S(2)}) copy-start(bf16[1,2,128,3,2,512]{5,2,4,3,1,0:T(8,128)(2,1)} %get-tuple-element.94) | copy-start | bytes 4718596
  201.3 5.0 %copy-start.9 = (bf16[1,2,128,3,2,512]{5,2,4,3,1,0:T(8,128)(2,1)S(1)}, bf16[1,2,128,3,2,512]{5,2,4,3,1,0:T(8,128)(2,1)}, u32[]{:S(2)}) copy-start(bf16[1,2,128,3,2,512]{5,2,4,3,1,0:T(8,128)(2,1)} %get-tuple-element.95) | copy-start | bytes 4718596
  201.3 13.0 %slice-start.2 = ((s8[6291456]{0:T(1024)(128)(4,1)}), s8[4194304]{0:T(1024)(128)(4,1)S(1)}, s32[]{:S(2)}) async-start(s8[6291456]{0:T(1024)(128)(4,1)} %bitcast.493), calls=%async_computation.9 | async-start | bytes 8388608
  206.3 8.1 %slice-start.3 = ((s8[6291456]{0:T(1024)(128)(4,1)}), s8[2097152]{0:T(1024)(128)(4,1)S(1)}, s32[]{:S(2)}) async-start(s8[6291456]{0:T(1024)(128)(4,1)} %bitcast.493), calls=%async_computation.10 | async-start | bytes 4194304
  211.2 114.4 %collective-permute-start.2 = (bf16[1024,3,2,256]{3,0,2,1:T(8,128)(2,1)}, bf16[1024,3,2,256]{3,0,2,1:T(8,128)(2,1)}, u32[]{:S(2)}, u32[]{:S(2)}) collective-permute-start(bf16[1024,3,2,256]{3,0,2,1:T(8,128)(2,1)} %get-tuple-element.30), channel_id=1, source_target_pairs={{0,1},{1,2},{2,3},{3,4},{4,5},{5,6},{6,7},{7,8},{8,9},{9,10},{10,1... | collective-permute-start | bytes 9437192 | tf_op jit(solution)/shard_map/ppermute | solution.py:23
  214.4 111.2 %collective-permute-start = (bf16[1024,3,2,256]{3,0,2,1:T(8,128)(2,1)}, bf16[1024,3,2,256]{3,0,2,1:T(8,128)(2,1)}, u32[]{:S(2)}, u32[]{:S(2)}) collective-permute-start(bf16[1024,3,2,256]{3,0,2,1:T(8,128)(2,1)} %get-tuple-element.31), channel_id=1, source_target_pairs={{1,0},{2,1},{3,2},{4,3},{5,4},{6,5},{7,6},{8,7},{9,8},{10,9},{11,1... | collective-permute-start | bytes 9437192 | tf_op jit(solution)/shard_map/ppermute | solution.py:25
  223.5 14.8 %slice-start.4 = ((s8[6291456]{0:T(1024)(128)(4,1)}), s8[2097152]{0:T(1024)(128)(4,1)S(1)}, s32[]{:S(2)}) async-start(s8[6291456]{0:T(1024)(128)(4,1)} %bitcast.495), calls=%async_computation.11 | async-start | bytes 4194304
  223.5 83.9 %all-to-all-start.2 = ((f32[16,2,2,8,1024]{4,3,1,2,0:T(8,128)}), f32[16,2,2,8,1024]{4,3,1,2,0:T(8,128)}, u32[]{:S(2)}, u32[]{:S(2)}) async-start(f32[16,2,2,8,1024]{4,3,1,2,0:T(8,128)} %bitcast.500), calls=%async_computation.2 | async-start | bytes 4194304 | tf_op jit(solution)/shard_map/all_to_all | solution.py:39
  230.9 7.3 %slice-start.5 = ((s8[6291456]{0:T(1024)(128)(4,1)}), s8[4194304]{0:T(1024)(128)(4,1)S(1)}, s32[]{:S(2)}) async-start(s8[6291456]{0:T(1024)(128)(4,1)} %bitcast.495), calls=%async_computation.12 | async-start | bytes 8388608
  243.5 69.0 %copy-start.20 = (f32[3,512]{1,0:T(4,128)S(1)}, f32[3,512]{1,0:T(4,128)}, u32[]{:S(2)}) copy-start(f32[3,512]{1,0:T(4,128)} %get-tuple-element.120) | copy-start | bytes 18436
  243.5 69.0 %copy-start.21 = (f32[3,512]{1,0:T(4,128)S(1)}, f32[3,512]{1,0:T(4,128)}, u32[]{:S(2)}) copy-start(f32[3,512]{1,0:T(4,128)} %get-tuple-element.121) | copy-start | bytes 18436
  243.5 69.0 %copy-start.22 = (f32[3,512]{1,0:T(4,128)S(1)}, f32[3,512]{1,0:T(4,128)}, u32[]{:S(2)}) copy-start(f32[3,512]{1,0:T(4,128)} %get-tuple-element.122) | copy-start | bytes 18436
  243.5 69.0 %copy-start.23 = (f32[3,512]{1,0:T(4,128)S(1)}, f32[3,512]{1,0:T(4,128)}, u32[]{:S(2)}) copy-start(f32[3,512]{1,0:T(4,128)} %get-tuple-element.117) | copy-start | bytes 18436
  243.6 69.0 %copy-start.24 = (f32[3,512]{1,0:T(4,128)S(1)}, f32[3,512]{1,0:T(4,128)}, u32[]{:S(2)}) copy-start(f32[3,512]{1,0:T(4,128)} %get-tuple-element.118) | copy-start | bytes 18436
  243.6 69.0 %copy-start.25 = (f32[3,512]{1,0:T(4,128)S(1)}, f32[3,512]{1,0:T(4,128)}, u32[]{:S(2)}) copy-start(f32[3,512]{1,0:T(4,128)} %get-tuple-element.119) | copy-start | bytes 18436
  307.3 33.6 %all-to-all-start.4 = ((f32[16,2,2,8,1024]{4,3,1,2,0:T(8,128)}), f32[16,2,2,8,1024]{4,3,1,2,0:T(8,128)}, u32[]{:S(2)}, u32[]{:S(2)}) async-start(f32[16,2,2,8,1024]{4,3,1,2,0:T(8,128)} %bitcast.451), calls=%async_computation.4 | async-start | bytes 4194304 | tf_op jit(solution)/shard_map/all_to_all | solution.py:39
  312.6 8.0 %copy-start.5 = (bf16[1,2,128,3,2,512]{5,2,4,3,1,0:T(8,128)(2,1)S(1)}, bf16[1,2,128,3,2,512]{5,2,4,3,1,0:T(8,128)(2,1)}, u32[]{:S(2)}) copy-start(bf16[1,2,128,3,2,512]{5,2,4,3,1,0:T(8,128)(2,1)} %get-tuple-element.94) | copy-start | bytes 4718596
  312.6 8.0 %copy-start.10 = (bf16[1,2,128,3,2,512]{5,2,4,3,1,0:T(8,128)(2,1)S(1)}, bf16[1,2,128,3,2,512]{5,2,4,3,1,0:T(8,128)(2,1)}, u32[]{:S(2)}) copy-start(bf16[1,2,128,3,2,512]{5,2,4,3,1,0:T(8,128)(2,1)} %get-tuple-element.95) | copy-start | bytes 4718596
  312.6 12.9 %slice-start = ((s8[6291456]{0:T(1024)(128)(4,1)}), s8[4194304]{0:T(1024)(128)(4,1)S(1)}, s32[]{:S(2)}) async-start(s8[6291456]{0:T(1024)(128)(4,1)} %bitcast.490), calls=%async_computation.7 | async-start | bytes 8388608
  330.1 17.1 %copy-start.14 = (f32[3,1,512]{2,0,1:T(4,128)S(1)}, f32[3,1,512]{2,0,1:T(4,128)}, u32[]{:S(2)}) copy-start(f32[3,1,512]{2,0,1:T(4,128)} %copy.159) | copy-start | bytes 18436
  330.1 17.1 %copy-start.15 = (f32[3,1,512]{2,0,1:T(4,128)S(1)}, f32[3,1,512]{2,0,1:T(4,128)}, u32[]{:S(2)}) copy-start(f32[3,1,512]{2,0,1:T(4,128)} %copy.160) | copy-start | bytes 18436
  330.1 17.1 %copy-start.16 = (f32[3,1,512]{2,0,1:T(4,128)S(1)}, f32[3,1,512]{2,0,1:T(4,128)}, u32[]{:S(2)}) copy-start(f32[3,1,512]{2,0,1:T(4,128)} %copy.161) | copy-start | bytes 18436
  330.1 17.1 %copy-start.17 = (f32[3,1,512]{2,0,1:T(4,128)S(1)}, f32[3,1,512]{2,0,1:T(4,128)}, u32[]{:S(2)}) copy-start(f32[3,1,512]{2,0,1:T(4,128)} %copy.162) | copy-start | bytes 18436
  330.1 17.1 %copy-start.18 = (f32[3,1,512]{2,0,1:T(4,128)S(1)}, f32[3,1,512]{2,0,1:T(4,128)}, u32[]{:S(2)}) copy-start(f32[3,1,512]{2,0,1:T(4,128)} %copy.163) | copy-start | bytes 18436
  330.1 17.1 %copy-start.19 = (f32[3,1,512]{2,0,1:T(4,128)S(1)}, f32[3,1,512]{2,0,1:T(4,128)}, u32[]{:S(2)}) copy-start(f32[3,1,512]{2,0,1:T(4,128)} %copy.164) | copy-start | bytes 18436
  341.0 34.4 %all-to-all-start.5 = ((f32[16,2,2,8,1024]{4,3,1,2,0:T(8,128)}), f32[16,2,2,8,1024]{4,3,1,2,0:T(8,128)}, u32[]{:S(2)}, u32[]{:S(2)}) async-start(f32[16,2,2,8,1024]{4,3,1,2,0:T(8,128)} %bitcast.501), calls=%async_computation.5 | async-start | bytes 4194304 | tf_op jit(solution)/shard_map/all_to_all | solution.py:39
  347.2 7.8 %copy-start.6 = (bf16[1,2,128,3,2,512]{5,2,4,3,1,0:T(8,128)(2,1)S(1)}, bf16[1,2,128,3,2,512]{5,2,4,3,1,0:T(8,128)(2,1)}, u32[]{:S(2)}) copy-start(bf16[1,2,128,3,2,512]{5,2,4,3,1,0:T(8,128)(2,1)} %get-tuple-element.94) | copy-start | bytes 4718596
  347.2 7.8 %copy-start.11 = (bf16[1,2,128,3,2,512]{5,2,4,3,1,0:T(8,128)(2,1)S(1)}, bf16[1,2,128,3,2,512]{5,2,4,3,1,0:T(8,128)(2,1)}, u32[]{:S(2)}) copy-start(bf16[1,2,128,3,2,512]{5,2,4,3,1,0:T(8,128)(2,1)} %get-tuple-element.95) | copy-start | bytes 4718596
  361.2 20.0 %copy-start.26 = (f32[3,512]{1,0:T(4,128)S(1)}, f32[3,512]{1,0:T(4,128)}, u32[]{:S(2)}) copy-start(f32[3,512]{1,0:T(4,128)} %get-tuple-element.114) | copy-start | bytes 18436
  361.2 20.0 %copy-start.27 = (f32[3,512]{1,0:T(4,128)S(1)}, f32[3,512]{1,0:T(4,128)}, u32[]{:S(2)}) copy-start(f32[3,512]{1,0:T(4,128)} %get-tuple-element.115) | copy-start | bytes 18436
  361.2 20.0 %copy-start.28 = (f32[3,512]{1,0:T(4,128)S(1)}, f32[3,512]{1,0:T(4,128)}, u32[]{:S(2)}) copy-start(f32[3,512]{1,0:T(4,128)} %get-tuple-element.116) | copy-start | bytes 18436
  361.2 20.0 %copy-start.29 = (f32[3,512]{1,0:T(4,128)S(1)}, f32[3,512]{1,0:T(4,128)}, u32[]{:S(2)}) copy-start(f32[3,512]{1,0:T(4,128)} %get-tuple-element.111) | copy-start | bytes 18436
  361.2 20.0 %copy-start.30 = (f32[3,512]{1,0:T(4,128)S(1)}, f32[3,512]{1,0:T(4,128)}, u32[]{:S(2)}) copy-start(f32[3,512]{1,0:T(4,128)} %get-tuple-element.112) | copy-start | bytes 18436
  361.2 20.0 %copy-start.31 = (f32[3,512]{1,0:T(4,128)S(1)}, f32[3,512]{1,0:T(4,128)}, u32[]{:S(2)}) copy-start(f32[3,512]{1,0:T(4,128)} %get-tuple-element.113) | copy-start | bytes 18436
  375.4 34.1 %all-to-all-start.3 = ((f32[16,2,2,8,1024]{4,3,1,2,0:T(8,128)}), f32[16,2,2,8,1024]{4,3,1,2,0:T(8,128)S(1)}, u32[]{:S(2)}, u32[]{:S(2)}) async-start(f32[16,2,2,8,1024]{4,3,1,2,0:T(8,128)} %bitcast.502), calls=%async_computation.3 | async-start | bytes 4194304 | tf_op jit(solution)/shard_map/all_to_all | solution.py:39
  381.2 7.8 %copy-start.7 = (bf16[1,2,128,3,2,512]{5,2,4,3,1,0:T(8,128)(2,1)S(1)}, bf16[1,2,128,3,2,512]{5,2,4,3,1,0:T(8,128)(2,1)}, u32[]{:S(2)}) copy-start(bf16[1,2,128,3,2,512]{5,2,4,3,1,0:T(8,128)(2,1)} %get-tuple-element.94) | copy-start | bytes 4718596
  381.2 7.8 %copy-start.12 = (bf16[1,2,128,3,2,512]{5,2,4,3,1,0:T(8,128)(2,1)S(1)}, bf16[1,2,128,3,2,512]{5,2,4,3,1,0:T(8,128)(2,1)}, u32[]{:S(2)}) copy-start(bf16[1,2,128,3,2,512]{5,2,4,3,1,0:T(8,128)(2,1)} %get-tuple-element.95) | copy-start | bytes 4718596
  409.5 34.2 %all-to-all-start.6 = ((f32[16,2,2,8,1024]{4,3,1,2,0:T(8,128)}), f32[16,2,2,8,1024]{4,3,1,2,0:T(8,128)}, u32[]{:S(2)}, u32[]{:S(2)}) async-start(f32[16,2,2,8,1024]{4,3,1,2,0:T(8,128)} %bitcast.503), calls=%async_computation.6 | async-start | bytes 4194304 | tf_op jit(solution)/shard_map/all_to_all | solution.py:39
  418.9 28.0 %copy-start.33 = (s32[6]{0:T(128)S(1)}, s32[6]{0:T(128)}, u32[]{:S(2)}) copy-start(s32[6]{0:T(128)} %param.6) | copy-start | bytes 76
  (4 other events, 17.5 us)
